TPU v7x, 512 devices: a whole 4x8x8 slice. The times are simulated.
512 devices in a mesh: grow: 16 (over y, core), gcol: 32 (over x, z).
Axes of the slice: x: 4, y: 8, z: 8, core: 2. Of those that a mesh axis runs over, the one named last changes fastest.
Arguments:
- pair_density: bfloat16 [16384, 2048], P('gcol', 'grow'), may hold values from -0.125 to 0.125
- pair_weight: float32 [2048], P('grow'), may hold values from 0.25 to 4
- coulomb: float32 [16384], replicated, may hold values from 0.25 to 4
- pivot_rows: int32 [512], replicated, may hold values from 0 to 16383, as said below
Outputs:
- dielectric: float32 [16384, 16384], P('grow', 'gcol')
- panel_factor: float32 [16384, 512], P('grow')
Inputs may be any that keep to these rules, and one draw needn't show every extreme that they name: `pivot_rows`: 512 distinct plane-wave indices, exactly one in each run of 32 consecutive plane waves starting at a multiple of it; 0 and 16383 are always among them.
All inputs are finite; a program needn't handle non-finite values.
Results may differ from a plain program's by a relative error of at most 0.0038.
Values may be sent and summed in bfloat16 or wider, within the bound.
A program may use at most 64 MiB of HBM per device.

v0:
```python
import jax
import jax.numpy as jnp
from jax import lax
from jax.sharding import Mesh
from jax.sharding import PartitionSpec as P

NG = 16384
PANEL = 512
GCOL = ("gcol_0", "gcol_1")
GROW = ("grow_0", "grow_1")


def joined_along(blocks, dim):
    lengths = list(blocks.shape[1:])
    lengths[dim] *= blocks.shape[0]
    return jnp.moveaxis(blocks, 0, dim).reshape(lengths)


def gather_in_order(x, axes, sequence):
    blocks = x
    for k in sequence:
        blocks = lax.all_gather(blocks, axes[k])
    done = sequence[::-1]
    back = [done.index(k) for k in range(len(axes))]
    blocks = blocks.transpose(*back, *range(len(axes), blocks.ndim))
    return blocks.reshape(-1, *x.shape)


def gather_axes(x, axes, sequence, dim):
    return joined_along(gather_in_order(x, axes, sequence), dim)


def sent_to_all(x, axis):
    length = lax.axis_size(axis)
    return lax.all_to_all(jnp.broadcast_to(x[None], (length, *x.shape)), axis, 0, 0, tiled=True)


def collect(x, axis, dim):
    return joined_along(sent_to_all(x, axis), dim)


def padded_to(lines, length):
    spare = -len(lines) % length
    return jnp.pad(lines, [(0, spare)] + [(0, 0)] * (lines.ndim - 1))


def reduced_to_own(blocks, axes, sequence):
    lengths = [lax.axis_size(a) for a in axes]
    blocks = blocks.reshape(*lengths, *blocks.shape[1:])
    blocks = blocks.transpose(*sequence, *range(len(axes), blocks.ndim))
    blocks = blocks.reshape(-1, *blocks.shape[len(axes) :])
    for k in sequence:
        blocks = lax.psum_scatter(blocks, axes[k], scatter_dimension=0, tiled=True)
    return blocks[0]


def sum_by_parts(x, axes, sequence):
    length, lines = (lax.axis_size(axes), x.reshape(-1, *x.shape[1:][-1:]))
    blocks = padded_to(lines, length).reshape(length, -1, *lines.shape[1:])
    own = reduced_to_own(blocks, axes, sequence)
    whole = gather_in_order(own, axes, sequence[::-1]).reshape(-1, *lines.shape[1:])
    return whole[: len(lines)].reshape(x.shape)


def factor_rows(columns_in, row_numbers, pivot_block, pivot_rows):
    width = pivot_rows.shape[0]
    factor = jnp.linalg.cholesky(pivot_block)
    pivot_diag = jnp.diagonal(factor)
    solved = lax.linalg.triangular_solve(
        factor, columns_in, left_side=False, lower=True, transpose_a=True
    )
    lower_part = solved / pivot_diag[None, :]
    upper = pivot_diag[:, None] * factor.T
    column_iota = lax.iota(jnp.int32, width)
    matches = row_numbers[:, None] == pivot_rows[None, :]
    is_pivot = jnp.any(matches, axis=1)
    position = jnp.sum(jnp.where(matches, column_iota[None, :], 0), axis=1)
    top_rows = jnp.take(upper, position, axis=0)
    upper_mask = is_pivot[:, None] & (column_iota[None, :] >= position[:, None])
    return jnp.where(upper_mask, top_rows, lower_part)


def select_rows(columns_in, first_row, pivot_rows):
    count_rows = columns_in.shape[0]
    offsets = pivot_rows - first_row
    inside = (offsets >= 0) & (offsets < count_rows)
    taken = jnp.take(columns_in, jnp.clip(offsets, 0, count_rows - 1), axis=0)
    return jnp.where(inside[:, None], taken, 0.0)


def body(pair_density, pair_weight, coulomb, pivot_rows):
    col_ratio = lax.axis_size(GCOL) // lax.axis_size(GROW)
    row_id = lax.axis_index(GROW)
    col_id = lax.axis_index(GCOL)
    scaled = (pair_density.astype(jnp.float32) * jnp.sqrt(pair_weight)[None, :]).astype(
        jnp.bfloat16
    )
    width_cols = scaled.shape[0]
    width_rows = width_cols * col_ratio
    contract = (((1,), (1,)), ((), ()))
    every_wave = gather_axes(scaled, GCOL, (0, 1), 0)
    row_side = lax.all_to_all(every_wave, GROW, split_axis=0, concat_axis=1, tiled=True)
    gram_block = lax.dot_general(
        row_side, collect(scaled, GROW, 1), contract, preferred_element_type=jnp.float32
    )
    first_global = row_id * width_rows
    row_numbers = first_global + lax.iota(jnp.int32, width_rows)
    col_numbers = col_id * width_cols + lax.iota(jnp.int32, width_cols)
    row_scale = jnp.sqrt(lax.dynamic_slice_in_dim(coulomb, first_global, width_rows))
    col_scale = jnp.sqrt(lax.dynamic_slice_in_dim(coulomb, col_id * width_cols, width_cols))
    identity = jnp.where(row_numbers[:, None] == col_numbers[None, :], 1.0, 0.0).astype(jnp.float32)
    dielectric = row_scale[:, None] * col_scale[None, :] * gram_block + identity
    stride = NG // PANEL
    per_device = width_cols // stride
    run_of = pivot_rows // stride
    run_pivot = jnp.zeros((PANEL,), jnp.int32).at[run_of].set(pivot_rows)
    local_cols = (
        lax.dynamic_slice_in_dim(run_pivot, col_id * per_device, per_device) - col_id * width_cols
    )
    own_columns = jnp.take(dielectric, local_cols, axis=1)
    run_columns = lax.all_gather(own_columns, GCOL, axis=1, tiled=True)
    columns = jnp.take(run_columns, run_of, axis=1)
    pivot_block = sum_by_parts(select_rows(columns, first_global, pivot_rows), GROW, (0, 1))
    panel_out = factor_rows(columns, row_numbers, pivot_block, pivot_rows)
    return (dielectric, panel_out)


def solution(mesh):
    finer = Mesh(mesh.devices.reshape(8, 2, 4, 8), ("grow_0", "grow_1", "gcol_0", "gcol_1"))
    return jax.shard_map(
        body,
        mesh=finer,
        in_specs=(P(GCOL, GROW), P(GROW), P(), P()),
        out_specs=(P(GROW, GCOL), P(GROW, None)),
        check_vma=False,
    )
```

profile of v0, /device:TPU:2, one launch (start us, length us, event | category | flops | bytes accessed | tf_op | source)
XLA Modules:
  0.0 581.8 jit_solution(7937591395494677095)
XLA Ops:
  8.8 16.2 %all-gather = bf16[2048,128]{1,0:T(8,128)(2,1)} all-gather(bf16[512,128]{1,0:T(8,128)(2,1)S(1)} %multiply_convert_fusion), channel_id=2, replica_groups=mesh['grow_0'=8,'grow_1'=2,'gcol_0'=4,'gcol_1'=8] {'gcol_0'}, dimensions={0}, use_global_device_ids=true | all-gather | bytes 655360 | tf_op jit(solution)/shard_map/all_gather | solution.py:22
  26.7 5.3 all-to-all-start.1
  32.0 53.7 %all-gather.9.cloned.1.call-done = bf16[32,512,128]{2,1,0:T(8,128)(2,1)} async-done(((bf16[4,512,128]{2,1,0:T(8,128)(2,1)}), bf16[32,512,128]{2,1,0:T(8,128)(2,1)}) %all-gather.9.cloned.1.call-update) | async-done | bytes 4194320 | tf_op jit(solution)/shard_map/all_gather | solution.py:22
  85.8 4.6 copy.20
  90.3 7.0 %all-to-all-start = ((bf16[16,1024,128]{2,1,0:T(8,128)(2,1)}), bf16[16,1024,128]{2,1,0:T(8,128)(2,1)}, u32[]{:S(2)}, u32[]{:S(2)}) async-start(bf16[16,1024,128]{2,1,0:T(8,128)(2,1)} %bitcast.81), calls=%async_computation | async-start | bytes 8388608 | tf_op jit(solution)/shard_map/all_to_all | solution.py:102
  101.5 90.2 %all-to-all-done = bf16[16,1024,128]{2,1,0:T(8,128)(2,1)} async-done(((bf16[16,1024,128]{2,1,0:T(8,128)(2,1)}), bf16[16,1024,128]{2,1,0:T(8,128)(2,1)}, u32[]{:S(2)}, u32[]{:S(2)}) %all-to-all-start) | async-done | bytes 4194336 | tf_op jit(solution)/shard_map/all_to_all | solution.py:102
  191.7 5.9 %fusion.4 = f32[1024,512]{1,0:T(8,128)} fusion(bf16[16,512,128]{2,1,0:T(8,128)(2,1)S(1)} %all-to-all-done.1, bf16[16,1024,128]{2,1,0:T(8,128)(2,1)} %all-to-all-done, s32[512]{0:T(512)S(1)} %iota_add_fusion.1, f32[512]{0:T(512)S(1)} %dynamic-slice_sqrt_fusion.1, f32[1024]{0:T(1024)S(1)} %dynamic-slice_sqrt_fusion, s32[1024]{0:T(1024)S(1)} %iota_add_fusion), kind=kOutput, calls=%fused_computation.16 | convolution fusion | flops 2150105088 | bytes 8400896 | tf_op jit(solution)/shard_map/dot_general | solution.py:103
  201.1 78.4 %all-gather.7.cloned.1.call-done = f32[1024,512]{0,1:T(8,128)} async-done(((f32[1024,16]{0,1:T(8,128)}), f32[1024,512]{0,1:T(8,128)}) %all-gather.7.cloned.1.call-update) | async-done | bytes 2097168 | tf_op jit(solution)/shard_map/all_gather | solution.py:121
  279.5 4.4 gather_fusion.1
  290.4 39.5 %reduce-scatter.3.cloned.1.call-done = f32[2,32,512]{2,1,0:T(8,128)} async-done(((f32[16,32,512]{2,1,0:T(8,128)}), f32[2,32,512]{2,1,0:T(8,128)}) %reduce-scatter.3.cloned.1.call-update) | async-done | bytes 131088 | tf_op jit(solution)/shard_map/reduce_scatter | solution.py:53
  330.0 17.3 %reduce-scatter.5.cloned.1.call-done = f32[1,32,512]{2,1,0:T(8,128)} async-done(((f32[2,32,512]{2,1,0:T(8,128)}), f32[1,32,512]{2,1,0:T(8,128)}) %reduce-scatter.5.cloned.1.call-update) | async-done | bytes 65552 | tf_op jit(solution)/shard_map/reduce_scatter | solution.py:53
  347.3 4.0 all_gather.29
  352.3 41.3 %all-gather.11.cloned.1.call-done = f32[16,32,512]{2,1,0:T(8,128)} async-done(((f32[2,32,512]{2,1,0:T(8,128)}), f32[16,32,512]{2,1,0:T(8,128)}) %all-gather.11.cloned.1.call-update) | async-done | bytes 1048592 | tf_op jit(solution)/shard_map/all_gather | solution.py:22
  398.6 11.7 %cholesky.102 = f32[128,128]{1,0:T(8,128)S(1)} custom-call(f32[128,128]{1,0:T(8,128)S(1)} %cholesky.260), custom_call_target="Cholesky" | custom-call | tf_op jit(solution)/shard_map/jit(cholesky)/cholesky | solution.py:67
  410.3 9.8 %custom-call.30 = f32[1,128,128]{1,2,0:T(8,128)S(1)} custom-call(f32[1,128,128]{2,1,0:T(8,128)S(1)} %get-tuple-element.43), custom_call_target="InvertDiagBlocksLowerTriangular" | custom-call | tf_op jit(solution)/shard_map/jit(cholesky)/cholesky | solution.py:67
  422.8 11.7 %cholesky.213 = f32[128,128]{1,0:T(8,128)S(1)} custom-call(f32[128,128]{1,0:T(8,128)S(1)} %cholesky.264), custom_call_target="Cholesky" | custom-call | tf_op jit(solution)/shard_map/jit(cholesky)/cholesky | solution.py:67
  434.6 9.9 %custom-call.31 = f32[1,128,128]{1,2,0:T(8,128)S(1)} custom-call(f32[1,128,128]{2,1,0:T(8,128)S(1)} %get-tuple-element.40), custom_call_target="InvertDiagBlocksLowerTriangular" | custom-call | tf_op jit(solution)/shard_map/jit(cholesky)/cholesky | solution.py:67
  446.1 11.7 %cholesky.234 = f32[128,128]{1,0:T(8,128)S(1)} custom-call(f32[128,128]{1,0:T(8,128)S(1)} %cholesky.269), custom_call_target="Cholesky" | custom-call | tf_op jit(solution)/shard_map/jit(cholesky)/cholesky | solution.py:67
  458.5 9.8 %custom-call.32 = f32[1,128,128]{1,2,0:T(8,128)S(1)} custom-call(f32[1,128,128]{2,1,0:T(8,128)S(1)} %get-tuple-element.37), custom_call_target="InvertDiagBlocksLowerTriangular" | custom-call | tf_op jit(solution)/shard_map/jit(cholesky)/cholesky | solution.py:67
  469.8 11.9 %cholesky.251 = f32[128,128]{1,0:T(8,128)S(1)} custom-call(f32[128,128]{1,0:T(8,128)S(1)} %convolution_subtract_fusion.4), custom_call_target="Cholesky" | custom-call | tf_op jit(solution)/shard_map/jit(cholesky)/cholesky | solution.py:67
  488.0 4.5 gather_fusion.3
  495.2 14.0 %while.1 = (s32[]{:T(128)}, f32[512,512]{1,0:T(8,128)}, s32[4,2]{0,1:T(2,128)S(1)}, f32[4,128,128]{2,1,0:T(8,128)}, s32[]{:T(128)}) while((s32[]{:T(128)}, f32[512,512]{1,0:T(8,128)}, s32[4,2]{0,1:T(2,128)S(1)}, f32[4,128,128]{2,1,0:T(8,128)}, s32[]{:T(128)}) %tuple.42), condition=%wide.while_cond, body=%wide.while_body.sunk | while | flops 2 | bytes 132205 | solution.py:69
  509.2 40.1 %custom-call.33 = f32[4,128,128]{1,2,0:T(8,128)S(1)} custom-call(f32[4,128,128]{2,1,0:T(8,128)} %get-tuple-element.9), custom_call_target="InvertDiagBlocksLowerTriangular" | custom-call | tf_op jit(solution)/shard_map/triangular_solve | solution.py:69
  560.5 4.9 gather_fusion.4
  (106 shorter events, 70.9 us)
Async XLA Ops:
  7.2 78.6 %all-gather.9.cloned.1.call-start = ((), (), s32[]{:S(2)}) async-start(), calls=%async_computation.7 | async-start | bytes 4718592 | tf_op jit(solution)/shard_map/all_gather | solution.py:22
  26.7 63.6 %all-to-all-start.1 = ((bf16[16,512,128]{2,1,0:T(8,128)(2,1)}), bf16[16,512,128]{2,1,0:T(8,128)(2,1)S(1)}, u32[]{:S(2)}, u32[]{:S(2)}) async-start(bf16[16,512,128]{2,1,0:T(8,128)(2,1)} %broadcast_in_dim.109), calls=%async_computation.1 | async-start | bytes 4194304 | tf_op jit(solution)/shard_map/all_to_all | solution.py:35
  90.3 7.1 %copy-start.9 = (s32[512]{0:T(512)S(1)}, s32[512]{0:T(512)}, u32[]{:S(2)}) copy-start(s32[512]{0:T(512)} %param.7) | copy-start | bytes 6148
  90.3 101.4 %all-to-all-start = ((bf16[16,1024,128]{2,1,0:T(8,128)(2,1)}), bf16[16,1024,128]{2,1,0:T(8,128)(2,1)}, u32[]{:S(2)}, u32[]{:S(2)}) async-start(bf16[16,1024,128]{2,1,0:T(8,128)(2,1)} %bitcast.81), calls=%async_computation | async-start | bytes 8388608 | tf_op jit(solution)/shard_map/all_to_all | solution.py:102
  97.4 182.1 %all-gather.7.cloned.1.call-start = ((), (), s32[]{:S(2)}) async-start(), calls=%async_computation.4 | async-start | bytes 2162688 | tf_op jit(solution)/shard_map/all_gather | solution.py:121
  200.9 129.1 %reduce-scatter.3.cloned.1.call-start = ((), (), s32[]{:S(2)}) async-start(), calls=%async_computation.5 | async-start | bytes 1179648 | tf_op jit(solution)/shard_map/reduce_scatter | solution.py:53
  290.4 57.0 %reduce-scatter.5.cloned.1.call-start = ((), (), s32[]{:S(2)}) async-start(), calls=%async_computation.6 | async-start | bytes 196608 | tf_op jit(solution)/shard_map/reduce_scatter | solution.py:53
  330.0 63.6 %all-gather.11.cloned.1.call-start = ((), (), s32[]{:S(2)}) async-start(), calls=%async_computation.8 | async-start | bytes 1179648 | tf_op jit(solution)/shard_map/all_gather | solution.py:22
  393.6 2.6 copy-start.7
  397.6 1.0 copy-start.8
  481.7 3.9 copy-start.4
  550.0 6.1 %copy-start = (f32[1024,128]{0,1:T(8,128)}, f32[1024,128]{0,1:T(8,128)S(1)}, u32[]{:S(2)}) copy-start(f32[1024,128]{0,1:T(8,128)S(1)} %fusion.25) | copy-start | bytes 1572868
  552.5 7.3 %copy-start.2 = (f32[1024,128]{0,1:T(8,128)}, f32[1024,128]{0,1:T(8,128)S(1)}, u32[]{:S(2)}) copy-start(f32[1024,128]{0,1:T(8,128)S(1)} %fusion.37) | copy-start | bytes 1572868
  556.0 3.8 copy-start.5
  565.4 3.1 copy-start.1
  565.4 3.1 copy-start.3
  565.4 3.1 copy-start.6
Sparse Core Ops, SparseCore 0:
  25.1 60.5 all-gather.8
  201.0 78.4 all-gather.6
  290.5 39.4 reduce-scatter.2
  332.6 14.7 reduce-scatter.4
  351.5 42.0 all-gather.10
where the time goes:
time: 588 us; the launch traced here: 582 us
  waiting for transfers between devices  321 us (55%)
  other arithmetic  133 us (23%)
  local copies, waits for them, and re-layouts  56 us (10%)
  matrix products  22.4 us (4%)
  blocking collectives  20.2 us (3%)
  between operations  16.8 us (3%)
  starting transfers between devices  12.5 us (2%)
    all_gather x2, waiting for transfers between devices, gather_in_order(): blocks = lax.all_gather(blocks, axes[k])  95 us
    all_to_all x1, waiting for transfers between devices, body(): lax.all_to_all(every_wave, GROW, split_axis=0, concat_axis=1, tiled=True)  90.2 us
    another operation x14, other arithmetic, factor_rows(): factor = jnp.linalg.cholesky(pivot_block)  78.9 us
    all_gather x1, waiting for transfers between devices, body(): run_columns = lax.all_gather(own_columns, GCOL, axis=1, tiled=True)  78.4 us
    reduce_scatter x2, waiting for transfers between devices, reduced_to_own(): blocks = lax.psum_scatter(blocks, axes[k], scatter_dimension=0, tiled=True)  56.8 us
    another operation x3, other arithmetic, factor_rows(): lax.linalg.triangular_solve(factor, columns_in, left_side=False, lower=Tr...  42.5 us
    all_gather x2, blocking collectives, gather_in_order(): blocks = lax.all_gather(blocks, axes[k])  20.2 us
    another operation x12, local copies, waits for them, and re-layouts  14 us
  transfers between devices with their start and end apart: 7, of which 6 were waited for; matrix products, arithmetic and copies ran while one was open for 2% of the time, Pallas kernels for 0%

commit v1 on v0

--- a/solution.py
+++ b/solution.py
@@ -118,7 +118,11 @@
         lax.dynamic_slice_in_dim(run_pivot, col_id * per_device, per_device) - col_id * width_cols
     )
     own_columns = jnp.take(dielectric, local_cols, axis=1)
-    run_columns = lax.all_gather(own_columns, GCOL, axis=1, tiled=True)
+    draft_flows = lambda u_in, mesh_dim: jnp.concatenate(
+        jax.lax.all_to_all(jnp.stack(jax.lax.axis_size(mesh_dim) * [u_in], 0), mesh_dim, 0, 0),
+        axis=1,
+    )
+    run_columns = draft_flows(own_columns, GCOL)
     columns = jnp.take(run_columns, run_of, axis=1)
     pivot_block = sum_by_parts(select_rows(columns, first_global, pivot_rows), GROW, (0, 1))
     panel_out = factor_rows(columns, row_numbers, pivot_block, pivot_rows)

time: 588 us -> 565 us (0.961)
  waiting for transfers between devices: 321 us -> 289 us
  starting transfers between devices: 12.5 us -> 19.7 us
    all_gather x1 -> x0, waiting for transfers between devices: 78.4 us -> none  [body(): run_columns = lax.all_gather(own_columns, GCOL, axis=1, tiled=True)]
    all_to_all x0 -> x1, waiting for transfers between devices: none -> 46.9 us  [body(): jax.lax.all_to_all(jnp.stack(jax.lax.axis_size(mesh_dim) * [u_in], 0), me...]
    all_to_all x0 -> x1, starting transfers between devices: none -> 7.27 us  [body(): jax.lax.all_to_all(jnp.stack(jax.lax.axis_size(mesh_dim) * [u_in], 0), me...]
    another operation x12 -> x13, local copies, waits for them, and re-layouts: 14 us -> 15.7 us
where the time goes in v1:
time: 565 us; the launch traced here: 558 us
  waiting for transfers between devices  289 us (51%)
  other arithmetic  133 us (24%)
  local copies, waits for them, and re-layouts  57 us (10%)
  matrix products  22.4 us (4%)
  blocking collectives  20.2 us (4%)
  starting transfers between devices  19.7 us (3%)
  between operations  16.9 us (3%)
    all_gather x2, waiting for transfers between devices, gather_in_order(): blocks = lax.all_gather(blocks, axes[k])  95 us
    all_to_all x1, waiting for transfers between devices, body(): lax.all_to_all(every_wave, GROW, split_axis=0, concat_axis=1, tiled=True)  90.3 us
    another operation x14, other arithmetic, factor_rows(): factor = jnp.linalg.cholesky(pivot_block)  78.9 us
    reduce_scatter x2, waiting for transfers between devices, reduced_to_own(): blocks = lax.psum_scatter(blocks, axes[k], scatter_dimension=0, tiled=True)  56.7 us
    all_to_all x1, waiting for transfers between devices, body(): jax.lax.all_to_all(jnp.stack(jax.lax.axis_size(mesh_dim) * [u_in], 0), me...  46.9 us
    another operation x3, other arithmetic, factor_rows(): lax.linalg.triangular_solve(factor, columns_in, left_side=False, lower=Tr...  42.5 us
    all_gather x2, blocking collectives, gather_in_order(): blocks = lax.all_gather(blocks, axes[k])  20.2 us
    another operation x12, local copies, waits for them, and re-layouts  14.1 us
  transfers between devices with their start and end apart: 7, of which 6 were waited for; matrix products, arithmetic and copies ran while one was open for 2% of the time, Pallas kernels for 0%

profile of v1, /device:TPU:2, one launch (start us, length us, event | category | flops | bytes accessed | tf_op | source)
XLA Modules:
  0.0 557.9 jit_solution(3179390964051111690)
XLA Ops:
  8.8 16.2 %all-gather = bf16[2048,128]{1,0:T(8,128)(2,1)} all-gather(bf16[512,128]{1,0:T(8,128)(2,1)S(1)} %multiply_convert_fusion), channel_id=2, replica_groups=mesh['grow_0'=8,'grow_1'=2,'gcol_0'=4,'gcol_1'=8] {'gcol_0'}, dimensions={0}, use_global_device_ids=true | all-gather | bytes 655360 | tf_op jit(solution)/shard_map/all_gather | solution.py:22
  26.7 5.3 all-to-all-start.1
  32.0 53.7 %all-gather.6.cloned.1.call-done = bf16[32,512,128]{2,1,0:T(8,128)(2,1)} async-done(((bf16[4,512,128]{2,1,0:T(8,128)(2,1)}), bf16[32,512,128]{2,1,0:T(8,128)(2,1)}) %all-gather.6.cloned.1.call-update) | async-done | bytes 4194320 | tf_op jit(solution)/shard_map/all_gather | solution.py:22
  85.8 4.6 copy.20
  90.3 7.0 %all-to-all-start = ((bf16[16,1024,128]{2,1,0:T(8,128)(2,1)}), bf16[16,1024,128]{2,1,0:T(8,128)(2,1)}, u32[]{:S(2)}, u32[]{:S(2)}) async-start(bf16[16,1024,128]{2,1,0:T(8,128)(2,1)} %bitcast.85), calls=%async_computation | async-start | bytes 8388608 | tf_op jit(solution)/shard_map/all_to_all | solution.py:102
  101.4 90.3 %all-to-all-done = bf16[16,1024,128]{2,1,0:T(8,128)(2,1)} async-done(((bf16[16,1024,128]{2,1,0:T(8,128)(2,1)}), bf16[16,1024,128]{2,1,0:T(8,128)(2,1)}, u32[]{:S(2)}, u32[]{:S(2)}) %all-to-all-start) | async-done | bytes 4194336 | tf_op jit(solution)/shard_map/all_to_all | solution.py:102
  191.7 5.9 %fusion.4 = f32[1024,512]{1,0:T(8,128)} fusion(bf16[16,512,128]{2,1,0:T(8,128)(2,1)S(1)} %all-to-all-done.1, bf16[16,1024,128]{2,1,0:T(8,128)(2,1)} %all-to-all-done, s32[512]{0:T(512)S(1)} %iota_add_fusion.1, f32[512]{0:T(512)S(1)} %dynamic-slice_sqrt_fusion.1, f32[1024]{0:T(1024)S(1)} %dynamic-slice_sqrt_fusion, s32[1024]{0:T(1024)S(1)} %iota_add_fusion), kind=kOutput, calls=%fused_computation.16 | convolution fusion | flops 2150105088 | bytes 8400896 | tf_op jit(solution)/shard_map/dot_general | solution.py:103
  201.8 7.3 %all-to-all-start.2 = ((f32[32,1024,16]{1,2,0:T(8,128)}), f32[32,1024,16]{1,2,0:T(8,128)S(1)}, u32[]{:S(2)}, u32[]{:S(2)}) async-start(f32[32,1024,16]{1,2,0:T(8,128)} %stack.2), calls=%async_computation.2 | async-start | bytes 4194304 | tf_op jit(solution)/shard_map/all_to_all | solution.py:122
  209.3 46.9 %all-to-all-done.2 = f32[32,1024,16]{1,2,0:T(8,128)S(1)} async-done(((f32[32,1024,16]{1,2,0:T(8,128)}), f32[32,1024,16]{1,2,0:T(8,128)S(1)}, u32[]{:S(2)}, u32[]{:S(2)}) %all-to-all-start.2) | async-done | bytes 2097184 | tf_op jit(solution)/shard_map/all_to_all | solution.py:122
  266.5 39.3 %reduce-scatter.3.cloned.1.call-done = f32[2,32,512]{2,1,0:T(8,128)} async-done(((f32[16,32,512]{2,1,0:T(8,128)}), f32[2,32,512]{2,1,0:T(8,128)}) %reduce-scatter.3.cloned.1.call-update) | async-done | bytes 131088 | tf_op jit(solution)/shard_map/reduce_scatter | solution.py:53
  305.9 17.5 %reduce-scatter.5.cloned.1.call-done = f32[1,32,512]{2,1,0:T(8,128)} async-done(((f32[2,32,512]{2,1,0:T(8,128)}), f32[1,32,512]{2,1,0:T(8,128)}) %reduce-scatter.5.cloned.1.call-update) | async-done | bytes 65552 | tf_op jit(solution)/shard_map/reduce_scatter | solution.py:53
  323.4 4.0 all_gather.25
  328.3 41.3 %all-gather.8.cloned.1.call-done = f32[16,32,512]{2,1,0:T(8,128)} async-done(((f32[2,32,512]{2,1,0:T(8,128)}), f32[16,32,512]{2,1,0:T(8,128)}) %all-gather.8.cloned.1.call-update) | async-done | bytes 1048592 | tf_op jit(solution)/shard_map/all_gather | solution.py:22
  374.6 11.7 %cholesky.102 = f32[128,128]{1,0:T(8,128)S(1)} custom-call(f32[128,128]{1,0:T(8,128)S(1)} %cholesky.260), custom_call_target="Cholesky" | custom-call | tf_op jit(solution)/shard_map/jit(cholesky)/cholesky | solution.py:67
  386.3 9.8 %custom-call.30 = f32[1,128,128]{1,2,0:T(8,128)S(1)} custom-call(f32[1,128,128]{2,1,0:T(8,128)S(1)} %get-tuple-element.43), custom_call_target="InvertDiagBlocksLowerTriangular" | custom-call | tf_op jit(solution)/shard_map/jit(cholesky)/cholesky | solution.py:67
  398.8 11.7 %cholesky.213 = f32[128,128]{1,0:T(8,128)S(1)} custom-call(f32[128,128]{1,0:T(8,128)S(1)} %cholesky.264), custom_call_target="Cholesky" | custom-call | tf_op jit(solution)/shard_map/jit(cholesky)/cholesky | solution.py:67
  410.6 9.9 %custom-call.31 = f32[1,128,128]{1,2,0:T(8,128)S(1)} custom-call(f32[1,128,128]{2,1,0:T(8,128)S(1)} %get-tuple-element.40), custom_call_target="InvertDiagBlocksLowerTriangular" | custom-call | tf_op jit(solution)/shard_map/jit(cholesky)/cholesky | solution.py:67
  422.1 11.7 %cholesky.234 = f32[128,128]{1,0:T(8,128)S(1)} custom-call(f32[128,128]{1,0:T(8,128)S(1)} %cholesky.269), custom_call_target="Cholesky" | custom-call | tf_op jit(solution)/shard_map/jit(cholesky)/cholesky | solution.py:67
  434.5 9.8 %custom-call.32 = f32[1,128,128]{1,2,0:T(8,128)S(1)} custom-call(f32[1,128,128]{2,1,0:T(8,128)S(1)} %get-tuple-element.37), custom_call_target="InvertDiagBlocksLowerTriangular" | custom-call | tf_op jit(solution)/shard_map/jit(cholesky)/cholesky | solution.py:67
  445.8 11.9 %cholesky.251 = f32[128,128]{1,0:T(8,128)S(1)} custom-call(f32[128,128]{1,0:T(8,128)S(1)} %convolution_subtract_fusion.4), custom_call_target="Cholesky" | custom-call | tf_op jit(solution)/shard_map/jit(cholesky)/cholesky | solution.py:67
  464.0 4.5 gather_fusion.3
  471.2 14.1 %while.1 = (s32[]{:T(128)}, f32[512,512]{1,0:T(8,128)}, s32[4,2]{0,1:T(2,128)S(1)}, f32[4,128,128]{2,1,0:T(8,128)}, s32[]{:T(128)}) while((s32[]{:T(128)}, f32[512,512]{1,0:T(8,128)}, s32[4,2]{0,1:T(2,128)S(1)}, f32[4,128,128]{2,1,0:T(8,128)}, s32[]{:T(128)}) %tuple.42), condition=%wide.while_cond, body=%wide.while_body.sunk | while | flops 2 | bytes 132205 | solution.py:69
  485.4 40.1 %custom-call.33 = f32[4,128,128]{1,2,0:T(8,128)S(1)} custom-call(f32[4,128,128]{2,1,0:T(8,128)} %get-tuple-element.9), custom_call_target="InvertDiagBlocksLowerTriangular" | custom-call | tf_op jit(solution)/shard_map/triangular_solve | solution.py:69
  536.6 4.9 gather_fusion.4
  (106 shorter events, 75.6 us)
Async XLA Ops:
  7.2 78.6 %all-gather.6.cloned.1.call-start = ((), (), s32[]{:S(2)}) async-start(), calls=%async_computation.7 | async-start | bytes 4718592 | tf_op jit(solution)/shard_map/all_gather | solution.py:22
  26.7 63.6 %all-to-all-start.1 = ((bf16[16,512,128]{2,1,0:T(8,128)(2,1)}), bf16[16,512,128]{2,1,0:T(8,128)(2,1)S(1)}, u32[]{:S(2)}, u32[]{:S(2)}) async-start(bf16[16,512,128]{2,1,0:T(8,128)(2,1)} %broadcast_in_dim.109), calls=%async_computation.1 | async-start | bytes 4194304 | tf_op jit(solution)/shard_map/all_to_all | solution.py:35
  90.3 7.0 %copy-start.9 = (s32[512]{0:T(512)S(1)}, s32[512]{0:T(512)}, u32[]{:S(2)}) copy-start(s32[512]{0:T(512)} %param.7) | copy-start | bytes 6148
  90.3 101.4 %all-to-all-start = ((bf16[16,1024,128]{2,1,0:T(8,128)(2,1)}), bf16[16,1024,128]{2,1,0:T(8,128)(2,1)}, u32[]{:S(2)}, u32[]{:S(2)}) async-start(bf16[16,1024,128]{2,1,0:T(8,128)(2,1)} %bitcast.85), calls=%async_computation | async-start | bytes 8388608 | tf_op jit(solution)/shard_map/all_to_all | solution.py:102
  201.8 54.5 %all-to-all-start.2 = ((f32[32,1024,16]{1,2,0:T(8,128)}), f32[32,1024,16]{1,2,0:T(8,128)S(1)}, u32[]{:S(2)}, u32[]{:S(2)}) async-start(f32[32,1024,16]{1,2,0:T(8,128)} %stack.2), calls=%async_computation.2 | async-start | bytes 4194304 | tf_op jit(solution)/shard_map/all_to_all | solution.py:122
  209.1 96.7 %reduce-scatter.3.cloned.1.call-start = ((), (), s32[]{:S(2)}) async-start(), calls=%async_computation.5 | async-start | bytes 1179648 | tf_op jit(solution)/shard_map/reduce_scatter | solution.py:53
  266.5 56.9 %reduce-scatter.5.cloned.1.call-start = ((), (), s32[]{:S(2)}) async-start(), calls=%async_computation.6 | async-start | bytes 196608 | tf_op jit(solution)/shard_map/reduce_scatter | solution.py:53
  305.8 63.8 %all-gather.8.cloned.1.call-start = ((), (), s32[]{:S(2)}) async-start(), calls=%async_computation.8 | async-start | bytes 1179648 | tf_op jit(solution)/shard_map/all_gather | solution.py:22
  369.6 2.6 copy-start.7
  373.6 1.0 copy-start.8
  457.7 4.0 copy-start.4
  526.1 6.1 %copy-start = (f32[1024,128]{0,1:T(8,128)}, f32[1024,128]{0,1:T(8,128)S(1)}, u32[]{:S(2)}) copy-start(f32[1024,128]{0,1:T(8,128)S(1)} %fusion.25) | copy-start | bytes 1572868
  528.7 7.3 %copy-start.2 = (f32[1024,128]{0,1:T(8,128)}, f32[1024,128]{0,1:T(8,128)S(1)}, u32[]{:S(2)}) copy-start(f32[1024,128]{0,1:T(8,128)S(1)} %fusion.37) | copy-start | bytes 1572868
  532.2 3.8 copy-start.5
  541.5 3.1 copy-start.1
  541.5 3.1 copy-start.3
  541.5 3.1 copy-start.6
Sparse Core Ops, SparseCore 0:
  25.1 60.5 all-gather.5
  266.6 39.1 reduce-scatter.2
  308.6 14.7 reduce-scatter.4
  327.5 42.0 all-gather.7
